TPU v7x, 32 devices: a whole 2x2x4 slice. The times are simulated.
32 devices in a mesh: grp: 2 (over x), gy: 4 (over z), gz: 4 (over y, core).
Axes of the slice: x: 2, y: 2, z: 4, core: 2. Of those that a mesh axis runs over, the one named last changes fastest.
Arguments:
- vorticity: float32 [2, 3, 256, 256, 256], P('grp', None, 'gz', 'gy'), may hold values from -6 to 6
- wind: float32 [2, 3], P('grp'), may hold values from 0.5 to 1.2
Outputs:
- new_vorticity: float32 [2, 3, 256, 256, 256], P('grp', None, 'gz', 'gy')
- velocity: float32 [2, 3, 256, 256, 256], P('grp', None, 'gz', 'gy')
All inputs are finite; a program needn't handle non-finite values.
Results may differ from a plain program's by a relative error of at most 0.0003.
Values sent between devices are 32-bit elements; how exact they have to be, the bound alone decides.
A program may use at most 192 MiB of HBM per device.

v0:
```python
import math

import jax
import jax.numpy as jnp
from jax import lax
from jax.sharding import PartitionSpec as P

TIME_STEP = 0.4
HIGHEST = lax.Precision.HIGHEST


def shifted(value, axis, steps):
    count = lax.axis_size(axis)
    initial, last = (max(0, -steps), min(count, count - steps))
    return lax.ppermute(value, axis, [(source, source + steps) for source in range(initial, last)])


def extended_2(cells, sides, width):
    for axis, dim in sides:
        count = lax.axis_size(axis)
        head = lax.slice_in_dim(cells, 0, width, axis=dim)
        tail = lax.slice_in_dim(cells, cells.shape[dim] - width, cells.shape[dim], axis=dim)
        cells = jnp.concatenate(
            [
                lax.ppermute(tail, axis, [(i, (i + 1) % count) for i in range(count)]),
                cells,
                lax.ppermute(head, axis, [((i + 1) % count, i) for i in range(count)]),
            ],
            axis=dim,
        )
    return cells


def kernel_weight(offset):
    mag = jnp.abs(offset)
    inner = 1.0 - 2.5 * mag * mag + 1.5 * mag * mag * mag
    outer = 0.5 * (2.0 - mag) * (2.0 - mag) * (1.0 - mag)
    return jnp.where(mag < 1.0, inner, jnp.where(mag < 2.0, outer, 0.0 * mag))


def tables(count):
    positions = jnp.arange(count, dtype=jnp.int32)
    product = positions[:, None] * positions[None, :] % count
    angles = product.astype(jnp.float32) * (2.0 * math.pi / count)
    return (jnp.cos(angles), jnp.sin(angles))


def apply_table(values, table, dim):
    letters = "abcd"
    output = letters[:dim] + "e" + letters[dim + 1 :]
    return jnp.einsum(
        letters + "," + letters[dim] + "e->" + output, values, table, precision=HIGHEST
    )


def transform(spectrum, dim, inverse):
    real_part = spectrum[:3]
    imag_part = spectrum[3:]
    count = spectrum.shape[dim + 1]
    cosine, sine_part = tables(count)
    real_cos = apply_table(real_part, cosine, dim + 1)
    real_sin = apply_table(real_part, sine_part, dim + 1)
    imag_cos = apply_table(imag_part, cosine, dim + 1)
    imag_sin = apply_table(imag_part, sine_part, dim + 1)
    if inverse:
        new_real = (real_cos - imag_sin) / count
        new_imag = (imag_cos + real_sin) / count
    else:
        new_real = real_cos + imag_sin
        new_imag = imag_cos - real_sin
    return jnp.concatenate([new_real, new_imag], 0)


def wave_numbers(index, count):
    signed = jnp.where(index < count // 2, index, index - count)
    return signed.astype(jnp.float32) * (2.0 * math.pi / count)


def odd_numbers(index, count):
    signed = jnp.where(index < count // 2, index, index - count)
    signed = jnp.where(index == count // 2, 0 * index, signed)
    return signed.astype(jnp.float32) * (2.0 * math.pi / count)


def curl_of(stream, wave_x, wave_y, wave_z):
    cross_x = wave_y * stream[2] - wave_z * stream[1]
    cross_y = wave_z * stream[0] - wave_x * stream[2]
    cross_z = wave_x * stream[1] - wave_y * stream[0]
    return jnp.stack([cross_x, cross_y, cross_z])


def reversed_lines(values):
    return jnp.roll(jnp.flip(values, (1, 2)), 1, (1, 2))


def curled_pair(real_in, imag_in, scaling, wave_y, wave_z):
    stream_real = real_in * scaling
    stream_imag = imag_in * scaling
    return (-curl_of(stream_imag, 0.0, wave_y, wave_z), curl_of(stream_real, 0.0, wave_y, wave_z))


def body(vorticity, wind):
    is_wake = lax.axis_index("grp") == 1
    field = vorticity[0]
    drift = wind[0]
    count_x = field.shape[3]
    half_x = count_x // 2
    cosine_x, sine_x = tables(count_x)
    alternate = 1.0 - 2.0 * (jnp.arange(count_x, dtype=jnp.int32) % 2).astype(jnp.float32)
    forward_cos = cosine_x[:, :half_x]
    forward_sin = jnp.concatenate([-alternate[:, None], sine_x[:, 1:half_x]], 1)
    real_part = jnp.einsum("czyx,xk->ckzy", field, forward_cos, precision=HIGHEST)
    imag_part = -jnp.einsum("czyx,xk->ckzy", field, forward_sin, precision=HIGHEST)
    spectrum = jnp.concatenate([real_part, imag_part], 0)
    size_gz = lax.axis_size("gz")
    spectrum = lax.all_to_all(spectrum, "gy", split_axis=1, concat_axis=3, tiled=True)
    spectrum = transform(spectrum, 2, False)
    spectrum = lax.all_to_all(spectrum, "gz", split_axis=1, concat_axis=2, tiled=True)
    spectrum = transform(spectrum, 1, False)
    owner = lax.axis_index("gy") * size_gz + lax.axis_index("gz")
    local_x = spectrum.shape[1]
    count_z = spectrum.shape[2]
    count_y = spectrum.shape[3]
    global_x = owner * local_x + jnp.arange(local_x, dtype=jnp.int32)
    index_z = jnp.arange(count_z, dtype=jnp.int32)
    index_y = jnp.arange(count_y, dtype=jnp.int32)
    wave_x = wave_numbers(global_x, count_x)[:, None, None]
    wave_z = wave_numbers(index_z, count_z)[None, :, None]
    wave_y = wave_numbers(index_y, count_y)[None, None, :]
    squared = wave_x * wave_x + wave_y * wave_y + wave_z * wave_z
    inverse = jnp.where(squared > 0, 1.0 / jnp.where(squared > 0, squared, 1.0), 0.0 * squared)
    curl_z = odd_numbers(index_z, count_z)[None, :, None]
    curl_y = odd_numbers(index_y, count_y)[None, None, :]
    stream_real = spectrum[:3] * inverse
    stream_imag = spectrum[3:] * inverse
    curled = jnp.concatenate(
        [
            -curl_of(stream_imag, wave_x, curl_y, curl_z),
            curl_of(stream_real, wave_x, curl_y, curl_z),
        ],
        0,
    )
    packed_plane = spectrum[:, 0]
    plain_real = packed_plane[:3]
    plain_imag = packed_plane[3:]
    mirror_real = reversed_lines(plain_real)
    mirror_imag = reversed_lines(plain_imag)
    base_real = 0.5 * (plain_real + mirror_real)
    base_imag = 0.5 * (plain_imag - mirror_imag)
    top_real = 0.5 * (plain_imag + mirror_imag)
    top_imag = -0.5 * (plain_real - mirror_real)
    plane_squared = wave_z[0] * wave_z[0] + wave_y[0] * wave_y[0]
    base_scale = jnp.where(
        plane_squared > 0,
        1.0 / jnp.where(plane_squared > 0, plane_squared, 1.0),
        0.0 * plane_squared,
    )
    top_scale = 1.0 / (plane_squared + math.pi * math.pi)
    base_vr, base_vi = curled_pair(base_real, base_imag, base_scale, curl_y[0], curl_z[0])
    top_vr, top_vi = curled_pair(top_real, top_imag, top_scale, curl_y[0], curl_z[0])
    rebuilt = jnp.concatenate([base_vr - top_vi, base_vi + top_vr], 0)
    chosen = jnp.where(global_x[0] == 0, rebuilt, curled[:, 0])
    curled = jnp.concatenate([chosen[:, None], curled[:, 1:]], 1)
    spectrum = curled
    spectrum = transform(spectrum, 1, True)
    spectrum = lax.all_to_all(spectrum, "gz", split_axis=2, concat_axis=1, tiled=True)
    spectrum = transform(spectrum, 2, True)
    spectrum = lax.all_to_all(spectrum, "gy", split_axis=3, concat_axis=1, tiled=True)
    back_cos = jnp.concatenate([cosine_x[:1], 2.0 * cosine_x[1:half_x]], 0)
    back_sin = jnp.concatenate([-alternate[None, :], 2.0 * sine_x[1:half_x]], 0)
    velocity = (
        jnp.einsum("ckzy,kx->czyx", spectrum[:3], back_cos, precision=HIGHEST)
        - jnp.einsum("ckzy,kx->czyx", spectrum[3:], back_sin, precision=HIGHEST)
    ) / count_x
    velocity = velocity + drift[:, None, None, None]
    planes = shifted(velocity[..., count_x - 2 :], "grp", 1)
    rimmed = extended_2(velocity, (("gz", 1), ("gy", 2)), 1)
    grad_z = (rimmed[:, 2:, 1:-1, :] - rimmed[:, :-2, 1:-1, :]) * 0.5
    grad_y = (rimmed[:, 1:-1, 2:, :] - rimmed[:, 1:-1, :-2, :]) * 0.5
    left_side = jnp.where(is_wake, planes[..., 1:], velocity[..., count_x - 1 :])
    right_side = jnp.where(is_wake, velocity[..., count_x - 1 :], velocity[..., :1])
    extended = jnp.concatenate([left_side, velocity, right_side], -1)
    grad_x = (extended[..., 2:] - extended[..., :-2]) * 0.5
    strength = field + TIME_STEP * (field[0:1] * grad_x + field[1:2] * grad_y + field[2:3] * grad_z)
    ghost = shifted(strength[..., count_x - 2 :], "grp", 1)
    shift_x = TIME_STEP * velocity[0]
    left_q = jnp.where(is_wake, ghost, strength[..., count_x - 2 :])
    left_d = jnp.where(is_wake, TIME_STEP * planes[0], shift_x[..., count_x - 2 :])
    right_q = jnp.where(is_wake, 0.0, strength[..., :2])
    right_d = jnp.where(is_wake, 0.0, shift_x[..., :2])
    q_ext = jnp.concatenate([left_q, strength, right_q], -1)
    d_ext = jnp.concatenate([left_d, shift_x, right_d], -1)
    moved = jnp.zeros_like(strength)
    for offset in range(-2, 3):
        start = 2 - offset
        moved = moved + q_ext[..., start : start + count_x] * kernel_weight(
            offset - d_ext[..., start : start + count_x]
        )
    packed = jnp.concatenate([moved, TIME_STEP * velocity[1:2]], 0)
    rim_rows = extended_2(packed, (("gy", 2),), 2)
    width_y = moved.shape[2]
    lateral = jnp.zeros_like(moved)
    for offset in range(-2, 3):
        start = 2 - offset
        lateral = lateral + rim_rows[:3, :, start : start + width_y, :] * kernel_weight(
            offset - rim_rows[3:4, :, start : start + width_y, :]
        )
    packed = jnp.concatenate([lateral, TIME_STEP * velocity[2:3]], 0)
    rim_cols = extended_2(packed, (("gz", 1),), 2)
    width_z = moved.shape[1]
    result = jnp.zeros_like(moved)
    for offset in range(-2, 3):
        start = 2 - offset
        result = result + rim_cols[:3, start : start + width_z, :, :] * kernel_weight(
            offset - rim_cols[3:4, start : start + width_z, :, :]
        )
    return (result[None], velocity[None])


def solution(mesh):
    return jax.shard_map(
        body,
        mesh=mesh,
        in_specs=(P("grp", None, "gz", "gy", None), P("grp", None)),
        out_specs=(P("grp", None, "gz", "gy", None), P("grp", None, "gz", "gy", None)),
        check_vma=False,
    )
```

profile of v0, /device:TPU:0, one launch (start us, length us, event | category | flops | bytes accessed | tf_op | source)
XLA Modules:
  0.0 1985.1 jit_solution(2008981749604816650)
XLA Ops:
  2.9 14.8 fusion.161
  17.7 12.1 negate_bitcast_fusion
  29.8 12.1 pad_maximum_fusion.14
  41.9 23.4 %copy.106 = f32[6,128,64,64]{3,2,0,1:T(8,128)} copy(f32[6,128,64,64]{1,3,2,0:T(8,128)} %pad_maximum_fusion.14) | data formatting | bytes 25165824 | tf_op jit(solution)/shard_map/concatenate | solution.py:114
  65.3 33.3 %reshape.530 = f32[4,1,786432]{2,1,0:T(1,128)} reshape(f32[128,6,64,64]{3,2,1,0:T(8,128)} %bitcast.250) | data formatting | bytes 25165824
  98.6 284.0 %all_to_all.60 = f32[4,1,786432]{2,1,0:T(1,128)} all-to-all(f32[4,1,786432]{2,1,0:T(1,128)} %reshape.530), channel_id=1, replica_groups=mesh['grp'=2,'gy'=4,'gz'=4] {'gy'}, dimensions={0} | all-to-all | bytes 25165824 | tf_op jit(solution)/shard_map/all_to_all | solution.py:116
  383.2 40.0 %reduce = f32[4,786432]{1,0:T(4,128)} reduce(f32[4,1,786432]{2,1,0:T(1,128)} %all_to_all.60, f32[]{:T(128)} %broadcast.847), dimensions={1}, to_apply=%all_to_all.44.reduce_sub_computation | reduce | bytes 25165828 | tf_op jit(solution)/shard_map/all_to_all | solution.py:116
  423.2 32.3 %reshape.531 = f32[128,6,64,64]{3,2,1,0:T(8,128)} reshape(f32[4,786432]{1,0:T(4,128)} %reduce) | data formatting | bytes 25165824
  455.5 17.7 copy.107
  473.2 14.7 fusion.317
  487.9 10.9 copy.108
  498.8 12.4 slice.405
  511.2 10.9 fusion.201
  522.1 16.4 copy.109
  538.5 12.5 slice.407
  551.1 10.9 fusion.199
  580.6 11.6 pad_maximum_fusion.15
  592.2 11.5 copy.110
  613.4 135.1 %all-to-all-done.1 = f32[6,32,64,256]{3,2,0,1:T(8,128)} async-done(((f32[6,32,64,256]{3,2,0,1:T(8,128)}), f32[6,32,64,256]{3,2,0,1:T(8,128)}, u32[]{:S(2)}, u32[]{:S(2)}) %all-to-all-start.1) | async-done | bytes 12582944 | tf_op jit(solution)/shard_map/all_to_all | solution.py:118
  748.5 11.5 copy.194
  786.2 11.9 broadcast_multiply_fusion
  880.5 16.6 copy.134
  897.2 147.4 %all_to_all.61 = f32[6,8,256,256]{3,1,0,2:T(8,128)} all-to-all(f32[6,8,256,256]{3,1,0,2:T(8,128)} %copy.134), channel_id=1, replica_groups=mesh['grp'=2,'gy'=4,'gz'=4] {'gz'}, dimensions={2} | all-to-all | bytes 25165824 | tf_op jit(solution)/shard_map/all_to_all | solution.py:166
  1044.5 16.6 copy.193
  1101.9 11.6 pad_maximum_fusion.17
  1113.5 23.5 %copy.136 = f32[6,32,64,256]{2,1,0,3:T(8,128)} copy(f32[6,32,64,256]{3,2,1,0:T(8,128)} %pad_maximum_fusion.17) | data formatting | bytes 25165824 | tf_op jit(solution)/shard_map/concatenate | solution.py:71
  1136.9 33.7 %reshape.532 = f32[4,1,786432]{2,1,0:T(1,128)} reshape(f32[256,6,32,64]{3,2,1,0:T(8,128)} %bitcast.252) | data formatting | bytes 25165824
  1187.3 262.6 %all-to-all-done.3 = f32[4,1,786432]{2,1,0:T(1,128)} async-done(((f32[4,1,786432]{2,1,0:T(1,128)}), f32[4,1,786432]{2,1,0:T(1,128)}, u32[]{:S(2)}, u32[]{:S(2)}) %all-to-all-start.3) | async-done | bytes 12582944 | tf_op jit(solution)/shard_map/all_to_all | solution.py:168
  1449.9 40.0 %reduce.1 = f32[4,786432]{1,0:T(4,128)} reduce(f32[4,1,786432]{2,1,0:T(1,128)} %all-to-all-done.3, f32[]{:T(128)} %broadcast.847), dimensions={1}, to_apply=%all_to_all.53.reduce_sub_computation | reduce | bytes 25165828 | tf_op jit(solution)/shard_map/all_to_all | solution.py:168
  1490.0 32.3 %reshape.533 = f32[256,6,32,64]{3,2,1,0:T(8,128)} reshape(f32[4,786432]{1,0:T(4,128)} %reduce.1) | data formatting | bytes 25165824
  1522.2 25.9 %copy.137 = f32[6,32,64,4,64]{4,2,1,3,0:T(8,128)} copy(f32[6,32,64,4,64]{2,1,0,4,3:T(8,128)} %bitcast.253) | data formatting | bytes 25165824 | tf_op jit(solution)/shard_map/all_to_all | solution.py:168
  1548.1 14.7 fusion.316
  1562.8 26.1 %fusion.34 = f32[3,64,64,256]{3,2,1,0:T(8,128)} fusion(f32[3,128,64,64]{3,2,1,0:T(8,128)S(1)} %bitcast.264, f32[127,256]{1,0:T(8,128)S(1)} %slice_multiply_fusion.11, f32[1,256]{1,0:T(1,128)S(1)} %fusion.245), kind=kOutput, calls=%fused_computation.70 | convolution fusion | flops 4831870976 | bytes 19005440 | tf_op jit(solution)/shard_map/ckzy,kx->czyx/dot_general | solution.py:173
  1588.9 33.2 %multiply_add_fusion = f32[3,64,64,256]{3,2,1,0:T(8,128)S(1)} fusion(f32[3,64,64,256]{3,2,1,0:T(8,128)} %fusion.34, f32[3]{0:T(128)S(1)} %bitcast.269, f32[3,128,64,64]{3,2,1,0:T(8,128)} %bitcast.260, f32[127,256]{1,0:T(8,128)S(1)} %slice_multiply_fusion.12, f32[1,256]{1,0:T(1,128)S(1)} %slice-done.10), kind=kOutput, calls=%fused_computation.76 | convolution fusion | flops 4841308160 | bytes 31588364 | tf_op jit(solution)/shard_map/ckzy,kx->czyx/dot_general | solution.py:172
  1628.8 12.1 fusion.121
  1656.3 12.9 slice_select_fusion.1
  1683.8 42.2 %fusion.23 = f32[3,64,64,256]{3,2,1,0:T(8,128)} fusion(f32[3,64,64,256]{3,2,1,0:T(8,128)} %copy-done, f32[3,1,64,256]{3,2,1,0:T(8,128)S(1)} %collective-permute-done.1, f32[3,1,64,256]{3,2,1,0:T(8,128)S(1)} %collective-permute-done.2, f32[3,66,1,256]{3,2,1,0:T(1,128)S(1)} %collective-permute-done.4, f32[3,66,1,256]{3,2,1,0:T(1,128)S(1)} %collective-permute-done.3, ...), kind=kLoop, calls=%fused_computation.42 | loop fusion | flops 62914560 | bytes 51228672 | tf_op jit(solution)/shard_map/add | solution.py:184
  1743.4 19.9 %fusion.52 = (f32[64,64,256]{2,1,0:T(8,128)}, f32[64,64,256]{2,1,0:T(8,128)}, f32[64,64,256]{2,1,0:T(8,128)}, f32[64,64,256]{2,1,0:T(8,128)}) fusion(f32[64,64,2]{2,1,0:T(8,128)S(1)} %get-tuple-element.62, f32[64,64,256]{2,1,0:T(8,128)} %get-tuple-element.32, f32[64,64,2]{2,1,0:T(8,128)} %get-tuple-element.63), kind=kLoop, calls=%fused_computation.151 | loop fusion | flops 83886080 | bytes 21037056 | tf_op jit(solution)/shard_map/jit(_where)/select_n | solution.py:38
  1767.6 11.6 slice_select_fusion
  1779.1 41.5 %fusion.3 = f32[3,64,64,256]{3,2,1,0:T(8,128)} fusion(f32[3,64,64,2]{3,2,1,0:T(8,128)} %get-tuple-element.35, f32[3,64,64,256]{3,2,1,0:T(8,128)} %fusion.23, f32[3,64,64,2]{3,2,1,0:T(8,128)} %get-tuple-element.34, f32[64,64,256]{2,1,0:T(8,128)} %get-tuple-element.60, f32[64,64,256]{2,1,0:T(8,128)} %get-tuple-element.61, ...), kind=kLoop, calls=%fused_computation.11 | loop fusion | flops 40894464 | bytes 46333952 | tf_op jit(solution)/shard_map/add | solution.py:196
  1836.3 11.9 collective-permute-done.7
  1848.2 13.3 fusion.79
  1861.6 13.1 pad_maximum_fusion
  1874.6 34.0 %fusion.13 = f32[3,64,64,256]{3,2,1,0:T(8,128)} fusion(f32[4,64,66,256]{3,2,1,0:T(8,128)} %get-tuple-element.23, f32[4,64,66,256]{3,2,1,0:T(8,128)} %get-tuple-element.22, f32[3,64,64,256]{3,2,1,0:T(8,128)} %fusion.3, f32[64,64,256]{2,1,0:T(8,128)} %get-tuple-element.20, f32[64,64,256]{2,1,0:T(8,128)} %get-tuple-element.21, ...), kind=kLoop, calls=%fused_computation.26 | loop fusion | flops 28311552 | bytes 96468992 | tf_op jit(solution)/shard_map/add | solution.py:205
  1910.7 11.5 collective-permute-done.8
  1924.6 11.6 fusion.109
  1936.2 15.7 pad_maximum_fusion.1
  1951.9 33.0 %fusion.9 = f32[1,3,64,64,256]{4,3,2,1,0:T(8,128)} fusion(f32[4,66,64,256]{3,2,1,0:T(8,128)} %get-tuple-element.17, f32[4,66,64,256]{3,2,1,0:T(8,128)} %get-tuple-element.16, f32[3,64,64,256]{3,2,1,0:T(8,128)} %fusion.13, f32[64,64,256]{2,1,0:T(8,128)} %get-tuple-element.14, f32[64,64,256]{2,1,0:T(8,128)} %get-tuple-element.15, ...), kind=kLoop, calls=%fused_computation.18 | loop fusion | flops 28311552 | bytes 96468992 | tf_op jit(solution)/shard_map/broadcast_in_dim | solution.py:217
  (169 shorter events, 274.9 us)
Async XLA Ops:
  1.6 16.1 copy-start.16
  2.6 15.1 copy-start.20
  2.8 14.8 copy-start.3
  538.5 23.5 %slice-start.8 = ((s8[6291456]{0:T(1024)(128)(4,1)}), s8[2097152]{0:T(1024)(128)(4,1)S(1)}, s32[]{:S(2)}) async-start(s8[6291456]{0:T(1024)(128)(4,1)} %bitcast.267), calls=%async_computation.12 | async-start | bytes 4194304
  551.1 10.9 copy-start.4
  551.1 11.0 slice-start.9
  551.1 20.1 %slice-start = ((s8[6291456]{0:T(1024)(128)(4,1)}), s8[4194304]{0:T(1024)(128)(4,1)S(1)}, s32[]{:S(2)}) async-start(s8[6291456]{0:T(1024)(128)(4,1)} %bitcast.240), calls=%async_computation.4 | async-start | bytes 8388608
  562.0 9.1 slice-start.1
  603.7 144.8 %all-to-all-start.1 = ((f32[6,32,64,256]{3,2,0,1:T(8,128)}), f32[6,32,64,256]{3,2,0,1:T(8,128)}, u32[]{:S(2)}, u32[]{:S(2)}) async-start(f32[6,32,64,256]{3,2,0,1:T(8,128)} %copy.110), calls=%async_computation.1 | async-start | bytes 25165824 | tf_op jit(solution)/shard_map/all_to_all | solution.py:118
  769.2 17.0 slice-start.4
  776.7 9.5 slice-start.5
  776.7 9.5 copy-start.9
  798.1 2.7 copy-start.11
  811.1 2.6 copy-start.10
  811.1 10.4 copy-start.19
  821.3 6.2 slice-start.6
  821.5 6.1 copy-start.8
  823.1 4.8 slice-start.7
  827.9 1.6 copy-start.13
  827.9 1.8 copy-start.18
  831.5 1.0 copy-start.22
  831.5 1.0 copy-start.23
  831.5 1.1 copy-start.24
  1070.3 6.5 slice-start.2
  1070.3 6.5 slice-start.3
  1170.6 6.5 copy-start.17
  1170.6 6.5 copy-start.21
  1170.6 279.3 %all-to-all-start.3 = ((f32[4,1,786432]{2,1,0:T(1,128)}), f32[4,1,786432]{2,1,0:T(1,128)}, u32[]{:S(2)}, u32[]{:S(2)}) async-start(f32[4,1,786432]{2,1,0:T(1,128)} %reshape.532), calls=%async_computation.3 | async-start | bytes 25165824 | tf_op jit(solution)/shard_map/all_to_all | solution.py:168
  1562.8 26.1 %slice-start.10 = ((f32[256,256]{1,0:T(8,128)}), f32[1,256]{1,0:T(1,128)S(1)}, s32[]{:S(2)}) async-start(f32[256,256]{1,0:T(8,128)} %copy-done.16), calls=%async_computation.14 | async-start | bytes 2048 | tf_op jit(solution)/shard_map/slice | solution.py:169
  1562.8 26.1 %copy-start.25 = (f32[1,3]{1,0:T(1,128)S(1)}, f32[1,3]{1,0:T(1,128)}, u32[]{:S(2)}) copy-start(f32[1,3]{1,0:T(1,128)} %param.3) | copy-start | bytes 40
  1622.1 6.7 copy-start
  1645.4 6.9 collective-permute-start
  1650.0 21.3 %collective-permute-start.2 = (f32[3,1,64,256]{3,2,1,0:T(8,128)S(1)}, f32[3,1,64,256]{3,2,1,0:T(8,128)S(1)}, u32[]{:S(2)}, u32[]{:S(2)}) collective-permute-start(f32[3,1,64,256]{3,2,1,0:T(8,128)S(1)} %get-tuple-element.41), channel_id=1, source_target_pairs={{1,0},{2,1},{3,2},{0,3},{5,4},{6,5},{7,6},{4,7},{9,8},{10,9},{11,1... | collective-permute-start | bytes 589832 | tf_op jit(solution)/shard_map/ppermute | solution.py:27
  1650.0 21.3 %collective-permute-start.1 = (f32[3,1,64,256]{3,2,1,0:T(8,128)S(1)}, f32[3,1,64,256]{3,2,1,0:T(8,128)S(1)}, u32[]{:S(2)}, u32[]{:S(2)}) collective-permute-start(f32[3,1,64,256]{3,2,1,0:T(8,128)S(1)} %get-tuple-element.42), channel_id=1, source_target_pairs={{0,1},{1,2},{2,3},{3,0},{4,5},{5,6},{6,7},{7,4},{8,9},{9,10},{10,1... | collective-permute-start | bytes 589832 | tf_op jit(solution)/shard_map/ppermute | solution.py:25
  1671.3 4.5 copy-start.7
  1671.3 4.5 copy-start.12
  1673.7 10.1 collective-permute-start.3
  1674.9 8.9 collective-permute-start.4
  1737.6 25.7 %collective-permute-start.5 = (f32[3,64,64,2]{2,1,3,0:T(8,128)S(1)}, f32[3,64,64,2]{2,1,3,0:T(8,128)S(1)}, u32[]{:S(2)}, u32[]{:S(2)}) collective-permute-start(f32[3,64,64,2]{2,1,3,0:T(8,128)S(1)} %copy.142), channel_id=1, source_target_pairs={{0,16},{1,17},{2,18},{3,19},{4,20},{5,21},{6,22},{7,23},{8,24},{9,... | collective-permute-start | bytes 294920 | tf_op jit(solution)/shard_map/ppermute | solution.py:15
  1820.6 27.6 %copy-start.1 = (f32[3,64,64,256]{3,2,1,0:T(8,128)S(1)}, f32[3,64,64,256]{3,2,1,0:T(8,128)}, u32[]{:S(2)}) copy-start(f32[3,64,64,256]{3,2,1,0:T(8,128)} %fusion.3) | copy-start | bytes 37748740
  1820.6 27.6 %copy-start.6 = (f32[1,64,64,256]{3,2,1,0:T(8,128)S(1)}, f32[1,64,64,256]{3,2,1,0:T(8,128)}, u32[]{:S(2)}) copy-start(f32[1,64,64,256]{3,2,1,0:T(8,128)} %get-tuple-element.31) | copy-start | bytes 12582916
  1823.4 12.9 collective-permute-start.6
  1824.0 24.2 %collective-permute-start.7 = (f32[4,64,2,256]{3,2,1,0:T(2,128)S(1)}, f32[4,64,2,256]{3,2,1,0:T(2,128)S(1)}, u32[]{:S(2)}, u32[]{:S(2)}) collective-permute-start(f32[4,64,2,256]{3,2,1,0:T(2,128)S(1)} %get-tuple-element.25), channel_id=1, source_target_pairs={{0,4},{4,8},{8,12},{12,0},{1,5},{5,9},{9,13},{13,1},{2,6},{6,10},{... | collective-permute-start | bytes 1572872 | tf_op jit(solution)/shard_map/ppermute | solution.py:25
  1908.6 16.0 copy-start.2
  1908.6 16.0 copy-start.5
  1910.1 12.1 collective-permute-start.8
  1910.2 13.6 collective-permute-start.9
  1922.2 1.6 copy-start.14
  (1 other events, 0.8 us)
where the time goes:
time: 2000 us; the launch traced here: 1990 us
  waiting for transfers between devices  441 us (22%)
  blocking collectives  431 us (22%)
  local copies, waits for them, and re-layouts  428 us (21%)
  other arithmetic  423 us (21%)
  matrix products  232 us (12%)
  starting transfers between devices  27.7 us (1%)
    all_to_all x1, blocking collectives, body(): lax.all_to_all(spectrum, 'gy', split_axis=1, concat_axis=3, tiled=True)  284 us
    all_to_all x1, waiting for transfers between devices, body(): lax.all_to_all(spectrum, 'gy', split_axis=3, concat_axis=1, tiled=True)  263 us
    all_to_all x1, blocking collectives, body(): lax.all_to_all(spectrum, 'gz', split_axis=2, concat_axis=1, tiled=True)  147 us
    dot_general x16, matrix products, apply_table(): jnp.einsum(letters + ',' + letters[dim] + 'e->' + output, values, table,...  146 us
    unnamed x76, local copies, waits for them, and re-layouts  140 us
    all_to_all x1, waiting for transfers between devices, body(): lax.all_to_all(spectrum, 'gz', split_axis=1, concat_axis=2, tiled=True)  135 us
    slice x5, local copies, waits for them, and re-layouts, transform(): real_part = spectrum[:3]  56.3 us
    concatenate x3, local copies, waits for them, and re-layouts, transform(): return jnp.concatenate([new_real, new_imag], 0)  51.6 us
  transfers between devices with their start and end apart: 12, of which 8 were waited for; matrix products, arithmetic and copies ran while one was open for 3% of the time, Pallas kernels for 0%

commit v1 on v0

--- a/solution.py
+++ b/solution.py
@@ -2,11 +2,12 @@
 
 import jax
 import jax.numpy as jnp
+import numpy as np
 from jax import lax
 from jax.sharding import PartitionSpec as P
 
 TIME_STEP = 0.4
-HIGHEST = lax.Precision.HIGHEST
+HIGH = lax.Precision.HIGH
 
 
 def shifted(value, axis, steps):
@@ -38,39 +39,6 @@
     return jnp.where(mag < 1.0, inner, jnp.where(mag < 2.0, outer, 0.0 * mag))
 
 
-def tables(count):
-    positions = jnp.arange(count, dtype=jnp.int32)
-    product = positions[:, None] * positions[None, :] % count
-    angles = product.astype(jnp.float32) * (2.0 * math.pi / count)
-    return (jnp.cos(angles), jnp.sin(angles))
-
-
-def apply_table(values, table, dim):
-    letters = "abcd"
-    output = letters[:dim] + "e" + letters[dim + 1 :]
-    return jnp.einsum(
-        letters + "," + letters[dim] + "e->" + output, values, table, precision=HIGHEST
-    )
-
-
-def transform(spectrum, dim, inverse):
-    real_part = spectrum[:3]
-    imag_part = spectrum[3:]
-    count = spectrum.shape[dim + 1]
-    cosine, sine_part = tables(count)
-    real_cos = apply_table(real_part, cosine, dim + 1)
-    real_sin = apply_table(real_part, sine_part, dim + 1)
-    imag_cos = apply_table(imag_part, cosine, dim + 1)
-    imag_sin = apply_table(imag_part, sine_part, dim + 1)
-    if inverse:
-        new_real = (real_cos - imag_sin) / count
-        new_imag = (imag_cos + real_sin) / count
-    else:
-        new_real = real_cos + imag_sin
-        new_imag = imag_cos - real_sin
-    return jnp.concatenate([new_real, new_imag], 0)
-
-
 def wave_numbers(index, count):
     signed = jnp.where(index < count // 2, index, index - count)
     return signed.astype(jnp.float32) * (2.0 * math.pi / count)
@@ -97,6 +65,43 @@
     stream_real = real_in * scaling
     stream_imag = imag_in * scaling
     return (-curl_of(stream_imag, 0.0, wave_y, wave_z), curl_of(stream_real, 0.0, wave_y, wave_z))
+
+
+def exchanged(pieces, axis):
+    count = lax.axis_size(axis)
+    received = [pieces[0]]
+    for step in range(1, count):
+        pairs = [(i, (i + step) % count) for i in range(count)]
+        received.append(lax.ppermute(pieces[step], axis, pairs))
+    return received
+
+
+def relative(table, dim, axis, sign):
+    count = lax.axis_size(axis)
+    table = jnp.asarray(table, jnp.float32)
+    steps = jnp.arange(count, dtype=jnp.int32)
+    order = (lax.axis_index(axis) + sign * steps) % count
+    return jnp.take(table, order, axis=dim)
+
+
+def angles(count):
+    positions = np.arange(count)
+    product = positions[:, None] * positions[None, :] % count
+    angle = product * (2.0 * np.pi / count)
+    return (np.cos(angle), np.sin(angle))
+
+
+def complex_table(count, inverse):
+    cosine, sine = angles(count)
+    if inverse:
+        cosine, sine = (cosine / count, -sine / count)
+    rows_real = np.stack([cosine, -sine], 1)
+    rows_imag = np.stack([sine, cosine], 1)
+    return np.stack([rows_real, rows_imag], 0)
+
+
+def dot(letters, values, table):
+    return jnp.einsum(letters, values, jnp.asarray(table, jnp.float32), precision=HIGH)
 
 
 def body(vorticity, wind):
@@ -105,22 +110,54 @@
     drift = wind[0]
     count_x = field.shape[3]
     half_x = count_x // 2
-    cosine_x, sine_x = tables(count_x)
-    alternate = 1.0 - 2.0 * (jnp.arange(count_x, dtype=jnp.int32) % 2).astype(jnp.float32)
+    size_gy = lax.axis_size("gy")
+    size_gz = lax.axis_size("gz")
+    local_y = field.shape[2]
+    count_y = local_y * size_gy
+    count_z = field.shape[1] * size_gz
+    cosine_x, sine_x = angles(count_x)
+    alternate = 1.0 - 2.0 * (np.arange(count_x) % 2)
     forward_cos = cosine_x[:, :half_x]
-    forward_sin = jnp.concatenate([-alternate[:, None], sine_x[:, 1:half_x]], 1)
-    real_part = jnp.einsum("czyx,xk->ckzy", field, forward_cos, precision=HIGHEST)
-    imag_part = -jnp.einsum("czyx,xk->ckzy", field, forward_sin, precision=HIGHEST)
-    spectrum = jnp.concatenate([real_part, imag_part], 0)
-    size_gz = lax.axis_size("gz")
-    spectrum = lax.all_to_all(spectrum, "gy", split_axis=1, concat_axis=3, tiled=True)
-    spectrum = transform(spectrum, 2, False)
-    spectrum = lax.all_to_all(spectrum, "gz", split_axis=1, concat_axis=2, tiled=True)
-    spectrum = transform(spectrum, 1, False)
+    forward_sin = np.concatenate([alternate[:, None], -sine_x[:, 1:half_x]], 1)
+    cosine_z, sine_z = angles(count_z)
+    table_y = complex_table(count_y, False)
+    table_y = table_y.reshape(2, size_gy, local_y, 2 * count_y)
+    table_y = table_y.transpose(1, 0, 2, 3).reshape(2 * count_y, 2 * count_y)
     owner = lax.axis_index("gy") * size_gz + lax.axis_index("gz")
+    share_x = half_x // (size_gy * size_gz)
+    local_z = field.shape[1]
+    split_x = (count_x, size_gy, size_gz, share_x)
+    forward_cos = relative(forward_cos.reshape(split_x), 2, "gz", 1).reshape(count_x, half_x)
+    forward_sin = relative(forward_sin.reshape(split_x), 2, "gz", 1).reshape(count_x, half_x)
+    split_z = (size_gz, local_z, count_z)
+    whole_z = (count_z, count_z)
+    forward_z = [relative(t.reshape(split_z), 0, "gz", -1).reshape(whole_z) for t in (cosine_z, sine_z)]
+    parts = []
+    for comp in range(3):
+        lines = jnp.concatenate(
+            [
+                dot("zyx,xk->kzy", field[comp], forward_cos),
+                dot("zyx,xk->kzy", field[comp], forward_sin),
+            ],
+            2,
+        )
+        lines = lax.all_to_all(lines, "gy", split_axis=0, concat_axis=2, tiled=True)
+        lines = dot("kzl,ln->kzn", lines, table_y)
+        pieces = [
+            lines[step * share_x : (step + 1) * share_x] for step in range(size_gz)
+        ]
+        lines = jnp.concatenate(exchanged(pieces, "gz"), 1)
+        real_in, imag_in = (lines[..., :count_y], lines[..., count_y:])
+        parts.append(
+            (
+                dot("kzy,zq->kqy", real_in, forward_z[0])
+                + dot("kzy,zq->kqy", imag_in, forward_z[1]),
+                dot("kzy,zq->kqy", imag_in, forward_z[0])
+                - dot("kzy,zq->kqy", real_in, forward_z[1]),
+            )
+        )
+    spectrum = jnp.stack([pair[0] for pair in parts] + [pair[1] for pair in parts])
     local_x = spectrum.shape[1]
-    count_z = spectrum.shape[2]
-    count_y = spectrum.shape[3]
     global_x = owner * local_x + jnp.arange(local_x, dtype=jnp.int32)
     index_z = jnp.arange(count_z, dtype=jnp.int32)
     index_y = jnp.arange(count_y, dtype=jnp.int32)
@@ -161,18 +198,43 @@
     rebuilt = jnp.concatenate([base_vr - top_vi, base_vi + top_vr], 0)
     chosen = jnp.where(global_x[0] == 0, rebuilt, curled[:, 0])
     curled = jnp.concatenate([chosen[:, None], curled[:, 1:]], 1)
-    spectrum = curled
-    spectrum = transform(spectrum, 1, True)
-    spectrum = lax.all_to_all(spectrum, "gz", split_axis=2, concat_axis=1, tiled=True)
-    spectrum = transform(spectrum, 2, True)
-    spectrum = lax.all_to_all(spectrum, "gy", split_axis=3, concat_axis=1, tiled=True)
-    back_cos = jnp.concatenate([cosine_x[:1], 2.0 * cosine_x[1:half_x]], 0)
-    back_sin = jnp.concatenate([-alternate[None, :], 2.0 * sine_x[1:half_x]], 0)
-    velocity = (
-        jnp.einsum("ckzy,kx->czyx", spectrum[:3], back_cos, precision=HIGHEST)
-        - jnp.einsum("ckzy,kx->czyx", spectrum[3:], back_sin, precision=HIGHEST)
-    ) / count_x
-    velocity = velocity + drift[:, None, None, None]
+    back_cos = np.concatenate([cosine_x[:1], 2.0 * cosine_x[1:half_x]], 0) / count_x
+    back_sin = np.concatenate([-alternate[None, :], 2.0 * sine_x[1:half_x]], 0) / -count_x
+    split_x = (size_gy, size_gz, share_x, count_x)
+    back_cos = relative(back_cos.reshape(split_x), 1, "gz", -1).reshape(half_x, count_x)
+    back_sin = relative(back_sin.reshape(split_x), 1, "gz", -1).reshape(half_x, count_x)
+    split_z = (count_z, size_gz, local_z)
+    cosine_z, sine_z = [
+        relative(t.reshape(split_z) / count_z, 1, "gz", 1).reshape(whole_z)
+        for t in (cosine_z, sine_z)
+    ]
+    table_y = complex_table(count_y, True)
+    table_y = table_y.reshape(2 * count_y, 2, size_gy, local_y)
+    table_y = table_y.transpose(2, 0, 1, 3).reshape(size_gy, 2 * count_y, 2 * local_y)
+    speeds = []
+    for comp in range(3):
+        real_in, imag_in = (curled[comp], curled[comp + 3])
+        lines = jnp.concatenate(
+            [
+                dot("kqy,qz->kzy", real_in, cosine_z) - dot("kqy,qz->kzy", imag_in, sine_z),
+                dot("kqy,qz->kzy", imag_in, cosine_z) + dot("kqy,qz->kzy", real_in, sine_z),
+            ],
+            2,
+        )
+        pieces = [
+            lines[:, step * local_z : (step + 1) * local_z] for step in range(size_gz)
+        ]
+        lines = jnp.concatenate(exchanged(pieces, "gz"), 0)
+        lines = jnp.concatenate(
+            [dot("kzn,nl->kzl", lines, table_y[side]) for side in range(size_gy)], 0
+        )
+        lines = lax.all_to_all(lines, "gy", split_axis=0, concat_axis=0, tiled=True)
+        speeds.append(
+            dot("kzy,kx->zyx", lines[..., :local_y], back_cos)
+            + dot("kzy,kx->zyx", lines[..., local_y:], back_sin)
+            + drift[comp]
+        )
+    velocity = jnp.stack(speeds)
     planes = shifted(velocity[..., count_x - 2 :], "grp", 1)
     rimmed = extended_2(velocity, (("gz", 1), ("gy", 2)), 1)
     grad_z = (rimmed[:, 2:, 1:-1, :] - rimmed[:, :-2, 1:-1, :]) * 0.5

time: 2000 us -> 1240 us (0.62)
  blocking collectives: 431 us -> 0 us
  local copies, waits for them, and re-layouts: 428 us -> 148 us
  other arithmetic: 423 us -> 339 us
  starting transfers between devices: 27.7 us -> 63 us
    all_to_all x2 -> x0, blocking collectives: 431 us -> none  [the longest x1 284 us: body(): lax.all_to_all(spectrum, 'gy', split_axis=1, concat_axis=3, tiled=True)]
    ppermute x0 -> x18, waiting for transfers between devices: none -> 151 us  [exchanged(): received.append(lax.ppermute(pieces[step], axis, pairs))]
    all_to_all x2 -> x6, waiting for transfers between devices: 398 us -> 265 us  [the longest x3 212 us: body(): lines = lax.all_to_all(lines, 'gy', split_axis=0, concat_axis=2, tiled=True)]
    unnamed x76 -> x114, local copies, waits for them, and re-layouts: 140 us -> 11.9 us
    all_to_all x2 -> x0, other arithmetic: 80 us -> none  [the longest x1 40 us: body(): lax.all_to_all(spectrum, 'gy', split_axis=1, concat_axis=3, tiled=True)]
    all_to_all x5 -> x0, local copies, waits for them, and re-layouts: 72.4 us -> none  [the longest x1 25.9 us: body(): lax.all_to_all(spectrum, 'gy', split_axis=3, concat_axis=1, tiled=True)]
    concatenate x4 -> x3, local copies, waits for them, and re-layouts: 75 us -> 16 us  [body(): jnp.concatenate([dot('zyx,xk->kzy', field[comp], forward_cos), dot('zyx,x...]
    slice x11 -> x16, local copies, waits for them, and re-layouts: 100 us -> 47.8 us  [the longest x9 22.9 us: body(): lines[:, step * local_z:(step + 1) * local_z]]
  transfers between devices with their start and end apart: 12 -> 34, of which waited for: 8 -> 23; matrix products, arithmetic and copies ran while one was open for 3% -> 24% of each run, Pallas kernels for 0% -> 0%
where the time goes in v1:
time: 1240 us; the launch traced here: 1230 us
  waiting for transfers between devices  456 us (37%)
  other arithmetic  339 us (27%)
  matrix products  223 us (18%)
  local copies, waits for them, and re-layouts  148 us (12%)
  starting transfers between devices  63 us (5%)
    dot_general x51, matrix products, dot(): jnp.einsum(letters, values, jnp.asarray(table, jnp.float32), precision=HIGH)  223 us
    all_to_all x3, waiting for transfers between devices, body(): lines = lax.all_to_all(lines, 'gy', split_axis=0, concat_axis=2, tiled=True)  212 us
    ppermute x18, waiting for transfers between devices, exchanged(): received.append(lax.ppermute(pieces[step], axis, pairs))  151 us
    all_to_all x3, waiting for transfers between devices, body(): lines = lax.all_to_all(lines, 'gy', split_axis=0, concat_axis=0, tiled=True)  52.8 us
    add x1, other arithmetic, body(): field + TIME_STEP * (field[0:1] * grad_x + field[1:2] * grad_y + field[2:...  48.6 us
    add x1, other arithmetic, body(): moved + q_ext[..., start:start + count_x] * kernel_weight(offset - d_ext[...  41.5 us
    broadcast_in_dim x2, other arithmetic, body(): return (result[None], velocity[None])  38.8 us
    add x1, other arithmetic, body(): lateral + rim_rows[:3, :, start:start + width_y, :] * kernel_weight(offse...  34 us
  transfers between devices with their start and end apart: 34, of which 23 were waited for; matrix products, arithmetic and copies ran while one was open for 24% of the time, Pallas kernels for 0%

profile of v1, /device:TPU:0, one launch (start us, length us, event | category | flops | bytes accessed | tf_op | source)
XLA Modules:
  0.0 1232.2 jit_solution(4995639777925526722)
XLA Ops:
  41.1 77.6 %all-to-all-done = f32[128,64,128]{2,1,0:T(8,128)} async-done(((f32[128,64,128]{2,1,0:T(8,128)}), f32[128,64,128]{2,1,0:T(8,128)}, u32[]{:S(2)}, u32[]{:S(2)}) %all-to-all-start) | async-done | bytes 4194336 | tf_op jit(solution)/shard_map/all_to_all | solution.py:144
  139.6 76.8 %all-to-all-done.1 = f32[128,64,128]{2,1,0:T(8,128)} async-done(((f32[128,64,128]{2,1,0:T(8,128)}), f32[128,64,128]{2,1,0:T(8,128)}, u32[]{:S(2)}, u32[]{:S(2)}) %all-to-all-start.1) | async-done | bytes 4194336 | tf_op jit(solution)/shard_map/all_to_all | solution.py:144
  244.7 11.4 collective-permute-done
  256.4 57.6 %all-to-all-done.2 = f32[128,64,128]{2,1,0:T(8,128)} async-done(((f32[128,64,128]{2,1,0:T(8,128)}), f32[128,64,128]{2,1,0:T(8,128)}, u32[]{:S(2)}, u32[]{:S(2)}) %all-to-all-start.2) | async-done | bytes 4194336 | tf_op jit(solution)/shard_map/all_to_all | solution.py:144
  332.6 13.3 %collective-permute-done.6 = f32[8,64,512]{2,1,0:T(8,128)S(1)} collective-permute-done((f32[8,64,512]{2,1,0:T(8,128)S(1)}, f32[8,64,512]{2,1,0:T(8,128)S(1)}, u32[]{:S(2)}, u32[]{:S(2)}) %collective-permute-start.6) | collective-permute-done | bytes 1048608 | tf_op jit(solution)/shard_map/ppermute | solution.py:75
  349.4 19.8 %collective-permute-done.8 = f32[8,64,512]{2,1,0:T(8,128)S(1)} collective-permute-done((f32[8,64,512]{2,1,0:T(8,128)S(1)}, f32[8,64,512]{2,1,0:T(8,128)S(1)}, u32[]{:S(2)}, u32[]{:S(2)}) %collective-permute-start.8) | collective-permute-done | bytes 1048608 | tf_op jit(solution)/shard_map/ppermute | solution.py:75
  432.2 14.5 %collective-permute-done.9 = f32[8,64,512]{2,1,0:T(8,128)} collective-permute-done((f32[8,64,512]{2,1,0:T(8,128)}, f32[8,64,512]{2,1,0:T(8,128)}, u32[]{:S(2)}, u32[]{:S(2)}) %collective-permute-start.9) | collective-permute-done | bytes 1048608 | tf_op jit(solution)/shard_map/ppermute | solution.py:75
  448.5 6.9 collective-permute-done.10
  458.6 13.0 %collective-permute-done.11 = f32[8,64,512]{2,1,0:T(8,128)} collective-permute-done((f32[8,64,512]{2,1,0:T(8,128)}, f32[8,64,512]{2,1,0:T(8,128)}, u32[]{:S(2)}, u32[]{:S(2)}) %collective-permute-start.11) | collective-permute-done | bytes 1048608 | tf_op jit(solution)/shard_map/ppermute | solution.py:75
  474.8 9.7 fusion.268
  491.2 6.7 fusion.266
  497.9 7.1 fusion.265
  540.6 12.6 %collective-permute-done.12 = f32[8,64,512]{2,1,0:T(8,128)} collective-permute-done((f32[8,64,512]{2,1,0:T(8,128)}, f32[8,64,512]{2,1,0:T(8,128)}, u32[]{:S(2)}, u32[]{:S(2)}) %collective-permute-start.12) | collective-permute-done | bytes 1048608 | tf_op jit(solution)/shard_map/ppermute | solution.py:75
  555.1 8.9 collective-permute-done.13
  567.1 13.0 %collective-permute-done.14 = f32[8,64,512]{2,1,0:T(8,128)} collective-permute-done((f32[8,64,512]{2,1,0:T(8,128)}, f32[8,64,512]{2,1,0:T(8,128)}, u32[]{:S(2)}, u32[]{:S(2)}) %collective-permute-start.14) | collective-permute-done | bytes 1048608 | tf_op jit(solution)/shard_map/ppermute | solution.py:75
  583.3 9.7 fusion.264
  593.1 6.7 fusion.263
  599.7 6.7 fusion.262
  606.4 7.1 fusion.261
  647.6 14.1 %collective-permute-done.15 = f32[8,64,512]{2,1,0:T(8,128)} collective-permute-done((f32[8,64,512]{2,1,0:T(8,128)S(1)}, f32[8,64,512]{2,1,0:T(8,128)}, u32[]{:S(2)}, u32[]{:S(2)}) %collective-permute-start.15) | collective-permute-done | bytes 1048608 | tf_op jit(solution)/shard_map/ppermute | solution.py:75
  663.5 7.2 collective-permute-done.16
  673.9 12.8 %collective-permute-done.17 = f32[8,64,512]{2,1,0:T(8,128)} collective-permute-done((f32[8,64,512]{2,1,0:T(8,128)}, f32[8,64,512]{2,1,0:T(8,128)}, u32[]{:S(2)}, u32[]{:S(2)}) %collective-permute-start.17) | collective-permute-done | bytes 1048608 | tf_op jit(solution)/shard_map/ppermute | solution.py:75
  689.9 9.7 fusion.260
  699.7 6.7 fusion.259
  713.1 7.1 fusion.257
  729.8 10.1 bitcast_multiply_fusion.2
  740.0 7.1 fusion.271
  747.1 7.0 fusion.160
  754.1 7.2 fusion.272
  761.3 7.2 fusion.156
  768.5 52.8 %all-to-all-done.5 = f32[128,64,128]{2,1,0:T(8,128)} async-done(((f32[128,64,128]{2,1,0:T(8,128)}), f32[128,64,128]{2,1,0:T(8,128)}, u32[]{:S(2)}, u32[]{:S(2)}) %all-to-all-start.5) | async-done | bytes 4194336 | tf_op jit(solution)/shard_map/all_to_all | solution.py:231
  845.4 12.2 fusion.42
  895.6 12.8 %slice_select_fusion.1 = (f32[3,64,64,1]{3,2,1,0:T(8,128)}, f32[3,64,64,1]{3,2,1,0:T(8,128)}) fusion(f32[3,64,64,256]{3,2,1,0:T(8,128)} %copy-done.5, pred[]{:T(512)S(6)} %eq.87, f32[3,64,64,1]{3,2,1,0:T(8,128)} %copy.335), kind=kLoop, calls=%fused_computation.87 | loop fusion | flops 24576 | bytes 245761 | tf_op jit(solution)/shard_map/jit(_where)/select_n | solution.py:243
  917.1 6.9 collective-permute-done.21
  924.0 48.6 %fusion.23 = f32[3,64,64,256]{3,2,1,0:T(8,128)} fusion(f32[3,1,64,256]{3,2,1,0:T(8,128)S(1)} %collective-permute-done.19, f32[1,64,64,256]{3,2,1,0:T(8,128)} %bitcast.339, f32[1,64,64,256]{3,2,1,0:T(8,128)} %bitcast.342, f32[1,64,64,256]{3,2,1,0:T(8,128)} %bitcast.345, f32[3,1,64,256]{3,2,1,0:T(8,128)S(1)} %collective-permute-done.20, ...), kind=kLoop, calls=%fused_computation.50 | loop fusion | flops 100663296 | bytes 51228672 | tf_op jit(solution)/shard_map/add | solution.py:246
  972.6 7.1 slice.707
  990.4 19.7 %fusion.32 = (f32[64,64,256]{2,1,0:T(8,128)}, f32[64,64,256]{2,1,0:T(8,128)}, f32[64,64,256]{2,1,0:T(8,128)}, f32[64,64,256]{2,1,0:T(8,128)}) fusion(f32[64,64,2]{2,1,0:T(8,128)S(1)} %get-tuple-element.62, f32[64,64,256]{2,1,0:T(8,128)} %get-tuple-element.65, f32[64,64,2]{2,1,0:T(8,128)} %get-tuple-element.63), kind=kLoop, calls=%fused_computation.161 | loop fusion | flops 83886080 | bytes 21037056 | tf_op jit(solution)/shard_map/jit(_where)/select_n | solution.py:39
  1014.3 11.5 slice_select_fusion
  1025.8 41.5 %fusion.3 = f32[3,64,64,256]{3,2,1,0:T(8,128)} fusion(f32[3,64,64,2]{3,2,1,0:T(8,128)} %get-tuple-element.31, f32[3,64,64,256]{3,2,1,0:T(8,128)} %fusion.23, f32[3,64,64,2]{3,2,1,0:T(8,128)} %get-tuple-element.30, f32[64,64,256]{2,1,0:T(8,128)} %get-tuple-element.60, f32[64,64,256]{2,1,0:T(8,128)} %get-tuple-element.61, ...), kind=kLoop, calls=%fused_computation.19 | loop fusion | flops 40894464 | bytes 46333952 | tf_op jit(solution)/shard_map/add | solution.py:258
  1077.4 6.7 collective-permute-done.24
  1084.2 11.0 collective-permute-done.25
  1095.2 13.1 %fusion.58 = (f32[64,64,256]{2,1,0:T(8,128)}, f32[64,64,256]{2,1,0:T(8,128)}, f32[64,64,256]{2,1,0:T(8,128)}, f32[64,64,256]{2,1,0:T(8,128)}) fusion(f32[4,64,2,256]{3,2,1,0:T(2,128)S(1)} %collective-permute-done.24, f32[1,64,64,256]{3,2,1,0:T(8,128)S(1)} %copy-done.7, f32[3,64,64,256]{3,2,1,0:T(8,128)S(1)} %bitcast.336, ...), kind=kLoop, calls=%fused_computation.187 | loop fusion | flops 88080384 | bytes 34603008 | tf_op jit(solution)/shard_map/mul | solution.py:267
  1108.3 13.1 %pad_maximum_fusion = (f32[4,64,66,256]{3,2,1,0:T(8,128)}, f32[4,64,66,256]{3,2,1,0:T(8,128)}) fusion(f32[4,64,2,256]{3,2,1,0:T(2,128)S(1)} %collective-permute-done.24, f32[1,64,64,256]{3,2,1,0:T(8,128)S(1)} %copy-done.7, f32[3,64,64,256]{3,2,1,0:T(8,128)S(1)} %bitcast.336, f32[4,64,2,256]{3,2,1,0:T(2,128)S(1)} %collective-permute-done.25), kind=kLoop, calls=%fused_computation.12 | loop fusion | flops 17301504 | bytes 52428800 | tf_op jit(solution)/shard_map/concatenate | solution.py:24
  1121.3 34.0 %fusion.13 = f32[3,64,64,256]{3,2,1,0:T(8,128)} fusion(f32[4,64,66,256]{3,2,1,0:T(8,128)} %get-tuple-element.23, f32[4,64,66,256]{3,2,1,0:T(8,128)} %get-tuple-element.22, f32[3,64,64,256]{3,2,1,0:T(8,128)} %fusion.3, f32[64,64,256]{2,1,0:T(8,128)} %get-tuple-element.20, f32[64,64,256]{2,1,0:T(8,128)} %get-tuple-element.21, ...), kind=kLoop, calls=%fused_computation.34 | loop fusion | flops 28311552 | bytes 96468992 | tf_op jit(solution)/shard_map/add | solution.py:267
  1157.6 10.7 collective-permute-done.26
  1171.6 11.6 fusion.87
  1183.3 15.5 %pad_maximum_fusion.1 = (f32[4,66,64,256]{3,2,1,0:T(8,128)}, f32[4,66,64,256]{3,2,1,0:T(8,128)}) fusion(f32[4,2,64,256]{3,2,1,0:T(8,128)} %copy-done.24, f32[1,64,64,256]{3,2,1,0:T(8,128)} %get-tuple-element.57, f32[3,64,64,256]{3,2,1,0:T(8,128)S(1)} %copy-done, f32[4,2,64,256]{3,2,1,0:T(8,128)} %copy-done.25), kind=kLoop, calls=%fused_computation.14 | loop fusion | flops 17301504 | bytes 52428800 | tf_op jit(solution)/shard_map/concatenate | solution.py:24
  1198.8 33.0 %fusion.9 = f32[1,3,64,64,256]{4,3,2,1,0:T(8,128)} fusion(f32[4,66,64,256]{3,2,1,0:T(8,128)} %get-tuple-element.17, f32[4,66,64,256]{3,2,1,0:T(8,128)} %get-tuple-element.16, f32[3,64,64,256]{3,2,1,0:T(8,128)} %fusion.13, f32[64,64,256]{2,1,0:T(8,128)} %get-tuple-element.14, f32[64,64,256]{2,1,0:T(8,128)} %get-tuple-element.15, ...), kind=kLoop, calls=%fused_computation.26 | loop fusion | flops 28311552 | bytes 96468992 | tf_op jit(solution)/shard_map/broadcast_in_dim | solution.py:279
  (307 shorter events, 392.8 us)
Async XLA Ops:
  0.7 223.3 %copy-start.45 = (pred[4]{0:T(512)(128)(4,1)}, pred[4]{0:T(512)(128)(4,1)S(1)}, u32[]{:S(2)}) copy-start(pred[4]{0:T(512)(128)(4,1)S(1)} %get-tuple-element.133) | copy-start | bytes 16
  18.8 99.8 %all-to-all-start = ((f32[128,64,128]{2,1,0:T(8,128)}), f32[128,64,128]{2,1,0:T(8,128)}, u32[]{:S(2)}, u32[]{:S(2)}) async-start(f32[128,64,128]{2,1,0:T(8,128)} %copy.238), calls=%async_computation | async-start | bytes 8388608 | tf_op jit(solution)/shard_map/all_to_all | solution.py:144
  118.6 97.8 %all-to-all-start.1 = ((f32[128,64,128]{2,1,0:T(8,128)}), f32[128,64,128]{2,1,0:T(8,128)}, u32[]{:S(2)}, u32[]{:S(2)}) async-start(f32[128,64,128]{2,1,0:T(8,128)} %copy.244), calls=%async_computation.1 | async-start | bytes 8388608 | tf_op jit(solution)/shard_map/all_to_all | solution.py:144
  139.6 81.7 %copy-start.40 = (f32[4,64,256]{2,1,0:T(8,128)S(1)}, f32[4,64,256]{2,1,0:T(8,128)}, u32[]{:S(2)}) copy-start(f32[4,64,256]{2,1,0:T(8,128)} %constant.182.clone2.1) | copy-start | bytes 786436
  139.6 82.3 %copy-start.39 = (f32[4,64,256]{2,1,0:T(8,128)S(1)}, f32[4,64,256]{2,1,0:T(8,128)}, u32[]{:S(2)}) copy-start(f32[4,64,256]{2,1,0:T(8,128)} %constant.181.clone2.1) | copy-start | bytes 786436
  139.6 82.9 %copy-start.38 = (f32[256,4,64]{0,2,1:T(8,128)S(1)}, f32[256,4,64]{0,2,1:T(8,128)}, u32[]{:S(2)}) copy-start(f32[256,4,64]{0,2,1:T(8,128)} %constant.187.clone2.1) | copy-start | bytes 786436
  139.6 83.4 %copy-start.37 = (f32[256,4,64]{0,2,1:T(8,128)S(1)}, f32[256,4,64]{0,2,1:T(8,128)}, u32[]{:S(2)}) copy-start(f32[256,4,64]{0,2,1:T(8,128)} %constant.186.clone2.1) | copy-start | bytes 786436
  216.4 97.6 %all-to-all-start.2 = ((f32[128,64,128]{2,1,0:T(8,128)}), f32[128,64,128]{2,1,0:T(8,128)}, u32[]{:S(2)}, u32[]{:S(2)}) async-start(f32[128,64,128]{2,1,0:T(8,128)} %copy.250), calls=%async_computation.2 | async-start | bytes 8388608 | tf_op jit(solution)/shard_map/all_to_all | solution.py:144
  232.3 23.7 %collective-permute-start = (f32[8,64,512]{2,1,0:T(8,128)S(1)}, f32[8,64,512]{2,1,0:T(8,128)}, u32[]{:S(2)}, u32[]{:S(2)}) collective-permute-start(f32[8,64,512]{2,1,0:T(8,128)S(1)} %get-tuple-element.87), channel_id=1, source_target_pairs={{0,1},{1,2},{2,3},{3,0},{4,5},{5,6},{6,7},{7,4},{8,9},{9,10},{10,1... | collective-permute-start | bytes 3145736 | tf_op jit(solution)/shard_map/ppermute | solution.py:75
  233.4 87.1 %collective-permute-start.1 = (f32[8,64,512]{2,1,0:T(8,128)}, f32[8,64,512]{2,1,0:T(8,128)}, u32[]{:S(2)}, u32[]{:S(2)}) collective-permute-start(f32[8,64,512]{2,1,0:T(8,128)} %get-tuple-element.86), channel_id=1, source_target_pairs={{0,2},{1,3},{2,0},{3,1},{4,6},{5,7},{6,4},{7,5},{8,10},{9,11},{10,... | collective-permute-start | bytes 3145736 | tf_op jit(solution)/shard_map/ppermute | solution.py:75
  234.9 85.6 %collective-permute-start.2 = (f32[8,64,512]{2,1,0:T(8,128)}, f32[8,64,512]{2,1,0:T(8,128)}, u32[]{:S(2)}, u32[]{:S(2)}) collective-permute-start(f32[8,64,512]{2,1,0:T(8,128)} %get-tuple-element.85), channel_id=1, source_target_pairs={{0,3},{1,0},{2,1},{3,2},{4,7},{5,4},{6,5},{7,6},{8,11},{9,8},{10,9... | collective-permute-start | bytes 3145736 | tf_op jit(solution)/shard_map/ppermute | solution.py:75
  244.2 81.4 %collective-permute-start.3 = (f32[8,64,512]{2,1,0:T(8,128)}, f32[8,64,512]{2,1,0:T(8,128)}, u32[]{:S(2)}, u32[]{:S(2)}) collective-permute-start(f32[8,64,512]{2,1,0:T(8,128)} %get-tuple-element.91), channel_id=1, source_target_pairs={{0,1},{1,2},{2,3},{3,0},{4,5},{5,6},{6,7},{7,4},{8,9},{9,10},{10,1... | collective-permute-start | bytes 3145736 | tf_op jit(solution)/shard_map/ppermute | solution.py:75
  244.2 82.8 %collective-permute-start.4 = (f32[8,64,512]{2,1,0:T(8,128)}, f32[8,64,512]{2,1,0:T(8,128)}, u32[]{:S(2)}, u32[]{:S(2)}) collective-permute-start(f32[8,64,512]{2,1,0:T(8,128)} %get-tuple-element.90), channel_id=1, source_target_pairs={{0,2},{1,3},{2,0},{3,1},{4,6},{5,7},{6,4},{7,5},{8,10},{9,11},{10,... | collective-permute-start | bytes 3145736 | tf_op jit(solution)/shard_map/ppermute | solution.py:75
  256.0 71.0 %collective-permute-start.5 = (f32[8,64,512]{2,1,0:T(8,128)}, f32[8,64,512]{2,1,0:T(8,128)}, u32[]{:S(2)}, u32[]{:S(2)}) collective-permute-start(f32[8,64,512]{2,1,0:T(8,128)} %get-tuple-element.89), channel_id=1, source_target_pairs={{0,3},{1,0},{2,1},{3,2},{4,7},{5,4},{6,5},{7,6},{8,11},{9,8},{10,9... | collective-permute-start | bytes 3145736 | tf_op jit(solution)/shard_map/ppermute | solution.py:75
  320.4 25.5 %collective-permute-start.6 = (f32[8,64,512]{2,1,0:T(8,128)S(1)}, f32[8,64,512]{2,1,0:T(8,128)S(1)}, u32[]{:S(2)}, u32[]{:S(2)}) collective-permute-start(f32[8,64,512]{2,1,0:T(8,128)S(1)} %get-tuple-element.95), channel_id=1, source_target_pairs={{0,1},{1,2},{2,3},{3,0},{4,5},{5,6},{6,7},{7,4},{8,9},{9,10},{10,1... | collective-permute-start | bytes 3145736 | tf_op jit(solution)/shard_map/ppermute | solution.py:75
  320.5 28.8 %collective-permute-start.7 = (f32[8,64,512]{2,1,0:T(8,128)S(1)}, f32[8,64,512]{2,1,0:T(8,128)S(1)}, u32[]{:S(2)}, u32[]{:S(2)}) collective-permute-start(f32[8,64,512]{2,1,0:T(8,128)S(1)} %get-tuple-element.94), channel_id=1, source_target_pairs={{0,2},{1,3},{2,0},{3,1},{4,6},{5,7},{6,4},{7,5},{8,10},{9,11},{10,... | collective-permute-start | bytes 3145736 | tf_op jit(solution)/shard_map/ppermute | solution.py:75
  325.5 43.6 %collective-permute-start.8 = (f32[8,64,512]{2,1,0:T(8,128)S(1)}, f32[8,64,512]{2,1,0:T(8,128)S(1)}, u32[]{:S(2)}, u32[]{:S(2)}) collective-permute-start(f32[8,64,512]{2,1,0:T(8,128)S(1)} %get-tuple-element.93), channel_id=1, source_target_pairs={{0,3},{1,0},{2,1},{3,2},{4,7},{5,4},{6,5},{7,6},{8,11},{9,8},{10,9... | collective-permute-start | bytes 3145736 | tf_op jit(solution)/shard_map/ppermute | solution.py:75
  425.1 21.6 %collective-permute-start.9 = (f32[8,64,512]{2,1,0:T(8,128)}, f32[8,64,512]{2,1,0:T(8,128)}, u32[]{:S(2)}, u32[]{:S(2)}) collective-permute-start(f32[8,64,512]{2,1,0:T(8,128)} %copy.280), channel_id=1, source_target_pairs={{0,1},{1,2},{2,3},{3,0},{4,5},{5,6},{6,7},{7,4},{8,9},{9,10},{10,1... | collective-permute-start | bytes 3145736 | tf_op jit(solution)/shard_map/ppermute | solution.py:75
  429.1 26.3 %collective-permute-start.10 = (f32[8,64,512]{2,1,0:T(8,128)}, f32[8,64,512]{2,1,0:T(8,128)}, u32[]{:S(2)}, u32[]{:S(2)}) collective-permute-start(f32[8,64,512]{2,1,0:T(8,128)} %copy.281), channel_id=1, source_target_pairs={{0,2},{1,3},{2,0},{3,1},{4,6},{5,7},{6,4},{7,5},{8,10},{9,11},{10,... | collective-permute-start | bytes 3145736 | tf_op jit(solution)/shard_map/ppermute | solution.py:75
  432.2 42.6 %copy-start.52 = (f32[512,128,1]{1,0,2:T(8,128)S(1)}, f32[512,128,1]{1,0,2:T(8,128)}, u32[]{:S(2)}) copy-start(f32[512,128,1]{1,0,2:T(8,128)} %constant.195) | copy-start | bytes 786436
  432.2 39.4 %collective-permute-start.11 = (f32[8,64,512]{2,1,0:T(8,128)}, f32[8,64,512]{2,1,0:T(8,128)}, u32[]{:S(2)}, u32[]{:S(2)}) collective-permute-start(f32[8,64,512]{2,1,0:T(8,128)} %copy.282), channel_id=1, source_target_pairs={{0,3},{1,0},{2,1},{3,2},{4,7},{5,4},{6,5},{7,6},{8,11},{9,8},{10,9... | collective-permute-start | bytes 3145736 | tf_op jit(solution)/shard_map/ppermute | solution.py:75
  507.3 108.5 %all-to-all-start.3 = ((f32[128,64,128]{2,1,0:T(8,128)}), f32[128,64,128]{2,1,0:T(8,128)}, u32[]{:S(2)}, u32[]{:S(2)}) async-start(f32[128,64,128]{2,1,0:T(8,128)} %pad_maximum_fusion.40), calls=%async_computation.3 | async-start | bytes 8388608 | tf_op jit(solution)/shard_map/all_to_all | solution.py:231
  532.8 20.4 %collective-permute-start.12 = (f32[8,64,512]{2,1,0:T(8,128)}, f32[8,64,512]{2,1,0:T(8,128)}, u32[]{:S(2)}, u32[]{:S(2)}) collective-permute-start(f32[8,64,512]{2,1,0:T(8,128)} %copy.302), channel_id=1, source_target_pairs={{0,1},{1,2},{2,3},{3,0},{4,5},{5,6},{6,7},{7,4},{8,9},{9,10},{10,1... | collective-permute-start | bytes 3145736 | tf_op jit(solution)/shard_map/ppermute | solution.py:75
  537.6 26.3 %collective-permute-start.13 = (f32[8,64,512]{2,1,0:T(8,128)}, f32[8,64,512]{2,1,0:T(8,128)}, u32[]{:S(2)}, u32[]{:S(2)}) collective-permute-start(f32[8,64,512]{2,1,0:T(8,128)} %copy.303), channel_id=1, source_target_pairs={{0,2},{1,3},{2,0},{3,1},{4,6},{5,7},{6,4},{7,5},{8,10},{9,11},{10,... | collective-permute-start | bytes 3145736 | tf_op jit(solution)/shard_map/ppermute | solution.py:75
  539.7 40.4 %collective-permute-start.14 = (f32[8,64,512]{2,1,0:T(8,128)}, f32[8,64,512]{2,1,0:T(8,128)}, u32[]{:S(2)}, u32[]{:S(2)}) collective-permute-start(f32[8,64,512]{2,1,0:T(8,128)} %copy.304), channel_id=1, source_target_pairs={{0,3},{1,0},{2,1},{3,2},{4,7},{5,4},{6,5},{7,6},{8,11},{9,8},{10,9... | collective-permute-start | bytes 3145736 | tf_op jit(solution)/shard_map/ppermute | solution.py:75
  615.8 106.7 %all-to-all-start.4 = ((f32[128,64,128]{2,1,0:T(8,128)}), f32[128,64,128]{2,1,0:T(8,128)}, u32[]{:S(2)}, u32[]{:S(2)}) async-start(f32[128,64,128]{2,1,0:T(8,128)} %pad_maximum_fusion.41), calls=%async_computation.4 | async-start | bytes 8388608 | tf_op jit(solution)/shard_map/all_to_all | solution.py:231
  640.3 21.3 %collective-permute-start.15 = (f32[8,64,512]{2,1,0:T(8,128)S(1)}, f32[8,64,512]{2,1,0:T(8,128)}, u32[]{:S(2)}, u32[]{:S(2)}) collective-permute-start(f32[8,64,512]{2,1,0:T(8,128)S(1)} %copy.322), channel_id=1, source_target_pairs={{0,1},{1,2},{2,3},{3,0},{4,5},{5,6},{6,7},{7,4},{8,9},{9,10},{10,1... | collective-permute-start | bytes 3145736 | tf_op jit(solution)/shard_map/ppermute | solution.py:75
  644.4 26.3 %collective-permute-start.16 = (f32[8,64,512]{2,1,0:T(8,128)}, f32[8,64,512]{2,1,0:T(8,128)}, u32[]{:S(2)}, u32[]{:S(2)}) collective-permute-start(f32[8,64,512]{2,1,0:T(8,128)} %copy.323), channel_id=1, source_target_pairs={{0,2},{1,3},{2,0},{3,1},{4,6},{5,7},{6,4},{7,5},{8,10},{9,11},{10,... | collective-permute-start | bytes 3145736 | tf_op jit(solution)/shard_map/ppermute | solution.py:75
  647.6 39.1 %collective-permute-start.17 = (f32[8,64,512]{2,1,0:T(8,128)}, f32[8,64,512]{2,1,0:T(8,128)}, u32[]{:S(2)}, u32[]{:S(2)}) collective-permute-start(f32[8,64,512]{2,1,0:T(8,128)} %copy.324), channel_id=1, source_target_pairs={{0,3},{1,0},{2,1},{3,2},{4,7},{5,4},{6,5},{7,6},{8,11},{9,8},{10,9... | collective-permute-start | bytes 3145736 | tf_op jit(solution)/shard_map/ppermute | solution.py:75
  661.7 28.2 %copy-start.53 = (f32[512,128,1]{1,0,2:T(8,128)S(1)}, f32[512,128,1]{1,0,2:T(8,128)}, u32[]{:S(2)}) copy-start(f32[512,128,1]{1,0,2:T(8,128)} %constant.195) | copy-start | bytes 786436
  722.5 98.8 %all-to-all-start.5 = ((f32[128,64,128]{2,1,0:T(8,128)}), f32[128,64,128]{2,1,0:T(8,128)}, u32[]{:S(2)}, u32[]{:S(2)}) async-start(f32[128,64,128]{2,1,0:T(8,128)} %pad_maximum_fusion.42), calls=%async_computation.5 | async-start | bytes 8388608 | tf_op jit(solution)/shard_map/all_to_all | solution.py:231
  837.7 25.7 %copy-start.4 = (f32[64,64,256]{2,1,0:T(8,128)}, f32[64,64,256]{2,1,0:T(8,128)S(1)}, u32[]{:S(2)}) copy-start(f32[64,64,256]{2,1,0:T(8,128)S(1)} %add_add_fusion.1) | copy-start | bytes 12582916
  882.9 8.5 collective-permute-start.18
  887.4 23.0 %collective-permute-start.19 = (f32[3,1,64,256]{3,2,1,0:T(8,128)S(1)}, f32[3,1,64,256]{3,2,1,0:T(8,128)S(1)}, u32[]{:S(2)}, u32[]{:S(2)}) collective-permute-start(f32[3,1,64,256]{3,2,1,0:T(8,128)S(1)} %get-tuple-element.38), channel_id=1, source_target_pairs={{0,1},{1,2},{2,3},{3,0},{4,5},{5,6},{6,7},{7,4},{8,9},{9,10},{10,1... | collective-permute-start | bytes 589832 | tf_op jit(solution)/shard_map/ppermute | solution.py:26
  888.0 22.4 %collective-permute-start.20 = (f32[3,1,64,256]{3,2,1,0:T(8,128)S(1)}, f32[3,1,64,256]{3,2,1,0:T(8,128)S(1)}, u32[]{:S(2)}, u32[]{:S(2)}) collective-permute-start(f32[3,1,64,256]{3,2,1,0:T(8,128)S(1)} %get-tuple-element.37), channel_id=1, source_target_pairs={{1,0},{2,1},{3,2},{0,3},{5,4},{6,5},{7,6},{4,7},{9,8},{10,9},{11,1... | collective-permute-start | bytes 589832 | tf_op jit(solution)/shard_map/ppermute | solution.py:28
  912.7 11.3 collective-permute-start.21
  914.1 9.9 collective-permute-start.22
  984.2 26.0 %collective-permute-start.23 = (f32[3,64,64,2]{2,1,3,0:T(8,128)S(1)}, f32[3,64,64,2]{2,1,3,0:T(8,128)S(1)}, u32[]{:S(2)}, u32[]{:S(2)}) collective-permute-start(f32[3,64,64,2]{2,1,3,0:T(8,128)S(1)} %copy.336), channel_id=1, source_target_pairs={{0,16},{1,17},{2,18},{3,19},{4,20},{5,21},{6,22},{7,23},{8,24},{9,... | collective-permute-start | bytes 294920 | tf_op jit(solution)/shard_map/ppermute | solution.py:16
  1067.3 27.9 %slice-start = ((s8[12582912]{0:T(1024)(128)(4,1)}), s8[4194304]{0:T(1024)(128)(4,1)S(1)}, s32[]{:S(2)}) async-start(s8[12582912]{0:T(1024)(128)(4,1)} %bitcast.335), calls=%async_computation.6 | async-start | bytes 8388608
  1067.3 27.9 %slice-start.1 = ((s8[12582912]{0:T(1024)(128)(4,1)}), s8[4194304]{0:T(1024)(128)(4,1)S(1)}, s32[]{:S(2)}) async-start(s8[12582912]{0:T(1024)(128)(4,1)} %bitcast.335), calls=%async_computation.7 | async-start | bytes 8388608
  1070.0 14.1 %collective-permute-start.24 = (f32[4,64,2,256]{3,2,1,0:T(2,128)S(1)}, f32[4,64,2,256]{3,2,1,0:T(2,128)S(1)}, u32[]{:S(2)}, u32[]{:S(2)}) collective-permute-start(f32[4,64,2,256]{3,2,1,0:T(2,128)S(1)} %get-tuple-element.24), channel_id=1, source_target_pairs={{4,0},{8,4},{12,8},{0,12},{5,1},{9,5},{13,9},{1,13},{6,2},{10,6},{... | collective-permute-start | bytes 1572872 | tf_op jit(solution)/shard_map/ppermute | solution.py:28
  1071.8 23.3 %slice-start.2 = ((s8[12582912]{0:T(1024)(128)(4,1)}), s8[4194304]{0:T(1024)(128)(4,1)S(1)}, s32[]{:S(2)}) async-start(s8[12582912]{0:T(1024)(128)(4,1)} %bitcast.335), calls=%async_computation.8 | async-start | bytes 8388608
  1071.8 23.3 %copy-start.7 = (f32[1,64,64,256]{3,2,1,0:T(8,128)S(1)}, f32[1,64,64,256]{3,2,1,0:T(8,128)}, u32[]{:S(2)}) copy-start(f32[1,64,64,256]{3,2,1,0:T(8,128)} %get-tuple-element.59) | copy-start | bytes 12582916
  1071.8 23.3 %collective-permute-start.25 = (f32[4,64,2,256]{3,2,1,0:T(2,128)S(1)}, f32[4,64,2,256]{3,2,1,0:T(2,128)S(1)}, u32[]{:S(2)}, u32[]{:S(2)}) collective-permute-start(f32[4,64,2,256]{3,2,1,0:T(2,128)S(1)} %get-tuple-element.25), channel_id=1, source_target_pairs={{0,4},{4,8},{8,12},{12,0},{1,5},{5,9},{9,13},{13,1},{2,6},{6,10},{... | collective-permute-start | bytes 1572872 | tf_op jit(solution)/shard_map/ppermute | solution.py:26
  1155.3 16.3 %copy-start = (f32[3,64,64,256]{3,2,1,0:T(8,128)S(1)}, f32[3,64,64,256]{3,2,1,0:T(8,128)}, u32[]{:S(2)}) copy-start(f32[3,64,64,256]{3,2,1,0:T(8,128)} %fusion.13) | copy-start | bytes 37748740
  1155.3 16.3 %copy-start.6 = (f32[1,64,64,256]{3,2,1,0:T(8,128)S(1)}, f32[1,64,64,256]{3,2,1,0:T(8,128)}, u32[]{:S(2)}) copy-start(f32[1,64,64,256]{3,2,1,0:T(8,128)} %get-tuple-element.57) | copy-start | bytes 12582916
  1156.8 11.5 collective-permute-start.26
  1156.9 13.9 %collective-permute-start.27 = (f32[4,2,64,256]{3,2,1,0:T(8,128)S(1)}, f32[4,2,64,256]{3,2,1,0:T(8,128)S(1)}, u32[]{:S(2)}, u32[]{:S(2)}) collective-permute-start(f32[4,2,64,256]{3,2,1,0:T(8,128)S(1)} %get-tuple-element.19), channel_id=1, source_target_pairs={{0,1},{1,2},{2,3},{3,0},{4,5},{5,6},{6,7},{7,4},{8,9},{9,10},{10,1... | collective-permute-start | bytes 1572872 | tf_op jit(solution)/shard_map/ppermute | solution.py:26
  (43 other events, 275.3 us)
